TPU v7x, 256 devices: a whole 4x4x8 slice. The times are simulated.
256 devices in a mesh: pipe: 8 (over x, y_lo), dp: 32 (over z, y_hi, core).
Axes of the slice: x: 4, y: 4 (y_hi: 2, y_lo: 2; y = y_hi * 2 + y_lo), z: 8, core: 2. Of those that a mesh axis runs over, the one named last changes fastest.
Arguments:
- master: float32 [8, 3, 3, 256, 256], P('pipe', None, None, 'dp'), may hold values from -6 to 6
- grad_acc: float32 [32, 8, 3, 3, 256, 256], P('dp', 'pipe'), may hold values from -6 to 6
- down_act: float32 [8, 32, 16, 32, 256], P('pipe', 'dp'), may hold values from -6 to 6
- down_next: float32 [32, 16, 32, 256], P('dp'), may hold values from -6 to 6
- up_stash: float32 [8, 32, 2, 16, 32, 256], P('pipe', 'dp'), may hold values from -6 to 6
- up_order: int32 [8, 32, 2], P('pipe', 'dp'), may hold values from 0 to 1, each once within a row
- up_grad: float32 [8, 32, 16, 32, 256], P('pipe', 'dp'), may hold values from -6 to 6
- up_next: float32 [32, 16, 32, 256], P('dp'), may hold values from -6 to 6
- ex_table: float32 [64], replicated, may hold values from 0.25 to 4
- ex_index: int32 [32], P('dp'), may hold values from 0 to 63
Outputs:
- down_out: float32 [8, 32, 16, 32, 256], P('pipe', 'dp')
- up_out: float32 [8, 32, 16, 32, 256], P('pipe', 'dp')
- new_master: float32 [8, 3, 3, 256, 256], P('pipe', None, None, 'dp')
Inputs may be any that keep to these rules, and one draw needn't show every extreme that they name: `up_order`: the two entries of a row of the last dimension differ.
All inputs are finite; a program needn't handle non-finite values.
Results may differ from a plain program's by a relative error of at most 0.0044.
Values may be sent and summed in bfloat16 or wider, within the bound.
No kernel may reach another device: no remote copies, remote signals or barrier semaphores. Data moves between devices by JAX's collectives and lax.ppermute only.
A program may use at most 128 MiB of HBM per device.

v0:
```python
import jax
import jax.numpy as jnp
from jax import lax
from jax.experimental import pallas as pl
from jax.experimental.pallas import tpu as pltpu
from jax.sharding import PartitionSpec as P


learning_rate = 0.05
PIPE, Z, Y, CORES = 8, 8, 2, 2
C, HT, WD = 256, 16, 32
PIX = HT * WD
PADDED = PIX + 2 * WD
TAPS = 9
SCALE = (9.0 * C) ** (-0.5)
bf16, f32 = jnp.bfloat16, jnp.float32
VM = pl.BlockSpec(memory_space=pltpu.VMEM)
SM = pl.BlockSpec(memory_space=pltpu.SMEM)


def moved(value, where):
    pairs = []
    for p in range(PIPE):
        for z in range(Z):
            for y in range(Y):
                for c in range(CORES):
                    to = where(p, z, y, c)
                    if to is None:
                        continue
                    tp, tz, ty, tc = to
                    if not 0 <= tp < PIPE:
                        continue
                    target = tp * 32 + (tz % Z) * 4 + ty * 2 + tc
                    pairs.append((p * 32 + z * 4 + y * 2 + c, target))
    return lax.ppermute(value, ("pipe", "dp"), pairs)


def to_core(value):
    return moved(value, lambda p, z, y, c: (p, z, y, 1 - c))


def to_y(value):
    return moved(value, lambda p, z, y, c: (p, z, 1 - y, c))


def to_mirror(value):
    return moved(value, lambda p, z, y, c: (PIPE - 1 - p, z, y, c))


def to_plane(value, flip, far):
    def where(p, z, y, c):
        return (PIPE - 1 - p if flip else p, z + 4 * far, y ^ c, c)

    return moved(value, where)


def to_owner(value, far):
    return moved(value, lambda p, z, y, c: (PIPE - 1 - p, z + 4 * (c ^ far), c, y))


def to_next(value):
    return moved(value, lambda p, z, y, c: (p + 1, z, y, c))


def to_z(value, k):
    return moved(value, lambda p, z, y, c: (p, z + k if c == 0 else z - k, y, c))


def place():
    dp = lax.axis_index("dp")
    return dp // 4, (dp // 2) % 2, dp % 2


def call(kernel, outs, args, specs=None, scratch=(), flops=0, after=()):
    specs = specs or [VM] * len(args)
    if after:
        used, body = len(args), kernel

        def kernel(*refs):
            body(*refs[:used], *refs[used + len(after) :])

    size = sum(a.size * a.dtype.itemsize for a in args) + sum(
        int(o.size) * o.dtype.itemsize for o in outs
    )
    return pl.pallas_call(
        kernel,
        out_shape=outs,
        in_specs=specs + [pl.BlockSpec(memory_space=pl.ANY)] * len(after),
        out_specs=[VM] * len(outs),
        scratch_shapes=list(scratch),
        compiler_params=pltpu.CompilerParams(vmem_limit_bytes=40 << 20),
        cost_estimate=pl.CostEstimate(flops=flops, bytes_accessed=size, transcendentals=0),
    )(*args, *after)


def shape(dims, dtype):
    return jax.ShapeDtypeStruct(dims, dtype)


def three_shifts(u):
    column = lax.broadcasted_iota(jnp.int32, u.shape, 0) % WD
    left = jnp.where(column == 0, 0.0, pltpu.roll(u, 1, 0))
    right = jnp.where(column == WD - 1, 0.0, pltpu.roll(u, PIX - 1, 0))
    return jnp.concatenate([left.astype(bf16), u.astype(bf16), right.astype(bf16)], axis=1)


def fill_padded(ref, value):
    edge = jnp.zeros((WD, value.shape[1]), value.dtype)
    ref[pl.ds(0, WD), :] = edge
    ref[pl.ds(WD, PIX), :] = value
    ref[pl.ds(WD + PIX, WD), :] = edge


def conv(col_ref, w_ref):
    total = None
    for a in range(3):
        part = jnp.dot(
            col_ref[pl.ds(a * WD, PIX), :],
            w_ref[pl.ds(3 * a, 3)].reshape(3 * C, C),
            preferred_element_type=f32,
        )
        total = part if total is None else total + part
    return total * SCALE


def conv_back(col_ref, w_ref):
    total = None
    for a in range(3):
        for b in range(3):
            part = lax.dot_general(
                col_ref[pl.ds((2 - a) * WD, PIX), pl.ds((2 - b) * C, C)],
                w_ref[3 * a + b],
                (((1,), (1,)), ((), ())),
                preferred_element_type=f32,
            )
            total = part if total is None else total + part
    return total * SCALE


def grads(xt_ref, dpad_ref, store):
    for a in range(3):
        g = jnp.dot(
            xt_ref[...], dpad_ref[pl.ds((2 - a) * WD, PIX), :], preferred_element_type=f32
        )
        for b in range(3):
            store(3 * a + b, (g[b * C : (b + 1) * C] * SCALE).reshape(Z * Y, 16, C))


def pair_kernel(own_ref, other_ref, pair_ref):
    _, _, core = place()
    mine, theirs = own_ref[...].astype(f32), other_ref[...].astype(f32)
    low, high = jnp.where(core == 0, mine, theirs), jnp.where(core == 0, theirs, mine)
    pair_ref[...] = jnp.concatenate([low, high], axis=1).astype(bf16)


def fill_plane(chunk_ref, half_ref, near, far):
    _, y, core = place()
    half = y ^ core
    chunk_ref[0, near[0]] = near[1][...]
    chunk_ref[0, 1 - near[0]] = near[2][...]
    chunk_ref[1, half] = far[0][...]
    chunk_ref[1, 1 - half] = far[1][...]
    for dz in range(2):
        half_ref[dz] = chunk_ref[dz, core]


def plane_mirror_kernel(near_ref, near_core_ref, far_ref, far_core_ref, chunk_ref, half_ref):
    _, y, core = place()
    fill_plane(chunk_ref, half_ref, (y ^ core, near_ref, near_core_ref), (far_ref, far_core_ref))


def plane_own_kernel(pair_ref, other_ref, far_ref, far_core_ref, chunk_ref, half_ref):
    _, y, _ = place()
    fill_plane(chunk_ref, half_ref, (y, pair_ref, other_ref), (far_ref, far_core_ref))


def assemble_kernel(chunk_ref, one_ref, one_core_ref, two_ref, two_core_ref, w_ref):
    z, _, core = place()
    sign = 2 * core - 1

    def put(source_z, source_y, value):
        w_ref[:, lax.rem(source_z + 2 * Z, Z) * 2 + source_y] = value

    for dz in range(2):
        for half in range(Y):
            put(z + 4 * dz, half, chunk_ref[dz, half])
            put(z + sign + 4 * dz, half, one_ref[dz, half])
            put(z - sign + 4 * dz, half, one_core_ref[dz, half])
        put(z + 2 * sign + 4 * dz, core, two_ref[dz])
        put(z - 2 * sign + 4 * dz, 1 - core, two_core_ref[dz])


def prep_kernel(u_ref, col_ref):
    fill_padded(col_ref, three_shifts(u_ref[...]))


def prep_stash_kernel(order_ref, stash_ref, col1_ref, xt1_ref, col2_ref, xt2_ref):
    for slot, col_ref, xt_ref in ((0, col1_ref, xt1_ref), (1, col2_ref, xt2_ref)):
        v3 = three_shifts(stash_ref[order_ref[0, slot]])
        fill_padded(col_ref, v3)
        xt_ref[...] = v3.T


def forward_first_kernel(col_ref, u_ref, w_ref, out_ref):
    pre = conv(col_ref, w_ref)
    out_ref[...] = (u_ref[...] + pre * jax.nn.sigmoid(pre)).astype(bf16)


def forward_second_kernel(arrived_ref, next_ref, w_ref, out_ref, col_ref):
    first = lax.axis_index("pipe") == 0
    u = jnp.where(first, next_ref[...], arrived_ref[...].astype(f32))
    fill_padded(col_ref, three_shifts(u))
    pre = conv(col_ref, w_ref)
    out_ref[...] = u + pre * jax.nn.sigmoid(pre)


def up_first_kernel(col_ref, g_ref, w_ref, back_ref, dpad_ref, dcol_ref):
    pre = conv(col_ref, w_ref)
    s = jax.nn.sigmoid(pre)
    g = g_ref[...]
    delta = (g * s * (1.0 + pre * (1.0 - s))).astype(bf16)
    fill_padded(dpad_ref, delta)
    fill_padded(dcol_ref, three_shifts(delta.astype(f32)))
    back_ref[...] = (g + conv_back(dcol_ref, w_ref)).astype(bf16)


def slope_kernel(col_ref, w_ref, slope_ref):
    pre = conv(col_ref, w_ref)
    s = jax.nn.sigmoid(pre)
    slope_ref[...] = s * (1.0 + pre * (1.0 - s))


def grad_first_kernel(xt_ref, dpad_ref, g_ref):
    def store(tap, value):
        g_ref[tap] = value

    grads(xt_ref, dpad_ref, store)


def share_out(total_ref, keep_ref, send_ref):
    z, _, core = place()
    sign = 1 - 2 * core

    def put(j, mine, theirs, mine_y, theirs_y):
        keep_ref[j] = total_ref[:, lax.rem(mine + 2 * Z, Z) * 2 + mine_y]
        send_ref[j] = total_ref[:, lax.rem(theirs + 2 * Z, Z) * 2 + theirs_y].astype(bf16)

    for dz in range(2):
        at = z + 4 * dz
        for half in range(Y):
            put(2 * dz + half, at + sign, at - sign, half, half)
        put(4 + dz, at + 2 * sign, at - 2 * sign, core, 1 - core)
        put(6 + dz, at, at, core, 1 - core)


def up_second_kernel(
    table_ref, index_ref, arrived_ref, next_ref, slope_ref, xt_ref, g_ref,
    keep_ref, send_ref, dpad_ref, cot_ref, total_ref,
):
    first = lax.axis_index("pipe") == 0
    factor = table_ref[index_ref[0]]
    cot = jnp.where(first, next_ref[...] * factor, arrived_ref[...].astype(f32))
    cot_ref[...] = cot
    fill_padded(dpad_ref, (cot * slope_ref[...]).astype(bf16))

    def store(tap, value):
        total_ref[tap] = g_ref[tap] + value

    grads(xt_ref, dpad_ref, store)
    share_out(total_ref, keep_ref, send_ref)


def up_out_kernel(cot_ref, dpad_ref, w_ref, out_ref, dcol_ref):
    delta = dpad_ref[pl.ds(WD, PIX), :].astype(f32)
    fill_padded(dcol_ref, three_shifts(delta))
    out_ref[...] = cot_ref[...] + conv_back(dcol_ref, w_ref)


def earlier_kernel(acc_ref, keep_ref, send_ref):
    share_out(acc_ref, keep_ref, send_ref)


def earlier_sum_kernel(keep_ref, got_ref, out_ref):
    out_ref[...] = (keep_ref[...] + got_ref[...].astype(f32)).astype(bf16)


def core_sum_kernel(keep_ref, got_ref, earlier_ref, one_ref, two_ref, mine_ref):
    def total(j):
        return keep_ref[j] + got_ref[j].astype(f32) + earlier_ref[j].astype(f32)

    for dz in range(2):
        for half in range(Y):
            one_ref[dz, half] = total(2 * dz + half).astype(bf16)
        two_ref[dz] = total(4 + dz).astype(bf16)
        mine_ref[dz] = total(6 + dz)


def z_sum_kernel(one_ref, two_ref, mine_ref, keep_ref, send_ref):
    _, _, core = place()
    for dz in range(2):
        keep_ref[dz] = mine_ref[dz] + two_ref[dz].astype(f32) + one_ref[dz, core].astype(f32)
        send_ref[dz] = one_ref[dz, 1 - core]


def z_core_sum_kernel(keep_ref, got_ref, near_ref, far_ref):
    _, _, core = place()
    for dz, out_ref in ((core, near_ref), (1 - core, far_ref)):
        out_ref[...] = (keep_ref[dz] + got_ref[dz].astype(f32)).astype(bf16)


def last_sum_kernel(a_ref, b_ref, keep_ref, send_ref, total_ref):
    _, _, core = place()
    total = a_ref[...].astype(f32) + b_ref[...].astype(f32)
    total_ref[...] = total.reshape(TAPS, CORES, 8, C)
    keep_ref[...] = total_ref[:, core]
    send_ref[...] = total_ref[:, 1 - core].astype(bf16)


CONV_FLOPS = 2 * PIX * TAPS * C * C
COL = shape((PADDED, 3 * C), bf16)
DPAD = shape((PADDED, C), bf16)
FIELD = shape((PIX, C), f32)
FIELD16 = shape((PIX, C), bf16)
COL_SCRATCH = pltpu.VMEM((PADDED, 3 * C), bf16)
TOTAL = shape((TAPS, Z * Y, 16, C), f32)
CHUNK = shape((2, Y, TAPS, 16, C), bf16)
HALF = shape((2, TAPS, 16, C), bf16)
PAIR = shape((TAPS, 16, C), bf16)


def assembled(chunk, half):
    one, two = to_z(chunk, 1), to_z(half, 2)
    args = [chunk, one, to_core(one), two, to_core(two)]
    w = call(assemble_kernel, [shape((TAPS, 16, 16, C), bf16)], args)[0]
    return w.reshape(TAPS, C, C)


def body(
    master, grad_acc, down_act, down_next, up_stash, up_order, up_grad, up_next, ex_table, ex_index
):
    own = master.reshape(TAPS, 8, C).astype(bf16)
    pair = call(pair_kernel, [PAIR], [own, to_core(own)])[0]

    far = to_plane(pair, True, 1)
    near = to_plane(pair, True, 0)
    chunk, half = call(plane_mirror_kernel, [CHUNK, HALF], [near, to_core(near), far, to_core(far)])
    w_mirror = assembled(chunk, half)

    own_other = to_y(pair)
    own_far = to_plane(pair, False, 1)
    act = down_act.reshape(PIX, C)
    stash = up_stash.reshape(2, PIX, C)
    col1, xt1, col2, xt2 = call(
        prep_stash_kernel, [COL, shape((3 * C, PIX), bf16)] * 2, [up_order[0], stash], [SM, VM]
    )
    col_down = call(prep_kernel, [COL], [act])[0]

    lists = [shape((8, TAPS, 16, C), f32), shape((8, TAPS, 16, C), bf16)]
    keep_e, send_e = call(earlier_kernel, lists, [grad_acc.reshape(TAPS, Z * Y, 16, C)])
    earlier = call(earlier_sum_kernel, lists[1:], [keep_e, to_core(send_e)])[0]
    earlier_moved = to_mirror(earlier)

    back, dpad1 = call(
        up_first_kernel,
        [FIELD16, DPAD],
        [col1, up_grad.reshape(PIX, C), w_mirror],
        scratch=[COL_SCRATCH],
        flops=2 * CONV_FLOPS,
    )
    passed = to_next(back)
    own_chunk, own_half = call(
        plane_own_kernel, [CHUNK, HALF], [pair, own_other, own_far, to_core(own_far)]
    )
    slope = call(slope_kernel, [FIELD], [col2, w_mirror], flops=CONV_FLOPS)[0]
    g1 = call(grad_first_kernel, [TOTAL], [xt1, dpad1], flops=CONV_FLOPS)[0]

    keep, send, dpad2, cot = call(
        up_second_kernel,
        lists + [DPAD, FIELD],
        [ex_table, ex_index, passed, up_next.reshape(PIX, C), slope, xt2, g1],
        [SM, SM, VM, VM, VM, VM, VM],
        scratch=[pltpu.VMEM((TAPS, Z * Y, 16, C), f32)],
        flops=CONV_FLOPS,
    )

    one, two, mine = call(
        core_sum_kernel, [CHUNK, HALF, shape(HALF.shape, f32)], [keep, to_core(send), earlier_moved]
    )
    got = [to_z(one, 1), to_z(two, 2)]

    w_own = assembled(own_chunk, own_half)
    section_out = call(forward_first_kernel, [FIELD16], [col_down, act, w_own], flops=CONV_FLOPS)[0]
    arrived = to_next(section_out)
    up_out = call(
        up_out_kernel, [FIELD], [cot, dpad2, w_mirror], scratch=[COL_SCRATCH], flops=CONV_FLOPS
    )[0]
    down_out = call(
        forward_second_kernel,
        [FIELD],
        [arrived, down_next.reshape(PIX, C), w_own],
        scratch=[COL_SCRATCH],
        flops=CONV_FLOPS,
    )[0]

    keep_z, send_z = call(z_sum_kernel, [shape(HALF.shape, f32), HALF], got + [mine])
    first, second = call(z_core_sum_kernel, [PAIR] * 2, [keep_z, to_core(send_z)])
    keep_l, send_l = call(
        last_sum_kernel,
        [shape((TAPS, 8, C), f32), shape((TAPS, 8, C), bf16)],
        [to_owner(first, 0), to_owner(second, 1)],
        scratch=[pltpu.VMEM((TAPS, CORES, 8, C), f32)],
    )
    got_l = to_core(send_l)
    total_grad = keep_l + got_l.astype(f32)
    new_master = master - learning_rate * total_grad.reshape(master.shape)
    field = (1, 1, HT, WD, C)
    return (down_out.reshape(field), up_out.reshape(field), new_master)


def solution(mesh):
    return jax.shard_map(
        body,
        mesh=mesh,
        in_specs=(
            P("pipe", None, None, "dp", None),
            P("dp", "pipe", None, None, None, None),
            P("pipe", "dp", None, None, None),
            P("dp", None, None, None),
            P("pipe", "dp", None, None, None, None),
            P("pipe", "dp", None),
            P("pipe", "dp", None, None, None),
            P("dp", None, None, None),
            P(),
            P("dp"),
        ),
        out_specs=(
            P("pipe", "dp", None, None, None),
            P("pipe", "dp", None, None, None),
            P("pipe", None, None, "dp", None),
        ),
        check_vma=False,
    )
```

profile of v0, /device:TPU:1, one launch (start us, length us, event | category | flops | bytes accessed | tf_op | source)
XLA Modules:
  0.0 120.5 jit_solution(9783418651229780455)
XLA Ops:
  1.5 3.2 %collective-permute-start = (bf16[9,8,256]{2,1,0:T(8,128)(2,1)S(1)}, bf16[9,8,256]{2,1,0:T(8,128)(2,1)S(1)}, u32[]{:S(2)}, u32[]{:S(2)}) collective-permute-start(bf16[9,8,256]{2,1,0:T(8,128)(2,1)S(1)} %bitcast.24), channel_id=1, source_target_pairs={{0,1},{1,0},{2,3},{3,2},{4,5},{5,4},{6,7},{7,6},{8,9},{9,8},{10,11... | collective-permute-start | bytes 110600 | tf_op jit(solution)/shard_map/ppermute | solution.py:35
  5.6 3.3 %collective-permute-start.9 = (bf16[9,16,256]{2,1,0:T(8,128)(2,1)S(1)}, bf16[9,16,256]{2,1,0:T(8,128)(2,1)S(1)}, u32[]{:S(2)}, u32[]{:S(2)}) collective-permute-start(bf16[9,16,256]{2,1,0:T(8,128)(2,1)S(1)} %shard_map.122.pair_ref), channel_id=1, source_target_pairs={{0,224},{1,227},{2,226},{3,225},{4,228},{5,231},{6,230},{7,229},{8... | collective-permute-start | bytes 221192 | tf_op jit(solution)/shard_map/ppermute | solution.py:35
  8.9 6.7 %collective-permute-start.11 = (bf16[9,16,256]{2,1,0:T(8,128)(2,1)S(1)}, bf16[9,16,256]{2,1,0:T(8,128)(2,1)S(1)}, u32[]{:S(2)}, u32[]{:S(2)}) collective-permute-start(bf16[9,16,256]{2,1,0:T(8,128)(2,1)S(1)} %shard_map.122.pair_ref), channel_id=1, source_target_pairs={{0,240},{1,243},{2,242},{3,241},{4,244},{5,247},{6,246},{7,245},{8... | collective-permute-start | bytes 221192 | tf_op jit(solution)/shard_map/ppermute | solution.py:35
  15.6 5.3 %collective-permute-done.11.far_ref = bf16[9,16,256]{2,1,0:T(8,128)(2,1)S(1)} collective-permute-done((bf16[9,16,256]{2,1,0:T(8,128)(2,1)S(1)}, bf16[9,16,256]{2,1,0:T(8,128)(2,1)S(1)}, u32[]{:S(2)}, u32[]{:S(2)}) %collective-permute-start.11) | collective-permute-done | bytes 73760 | tf_op jit(solution)/shard_map/ppermute | solution.py:35
  22.3 5.7 %collective-permute-start.13 = (bf16[2,2,9,16,256]{4,3,2,1,0:T(8,128)(2,1)S(1)}, bf16[2,2,9,16,256]{4,3,2,1,0:T(8,128)(2,1)S(1)}, u32[]{:S(2)}, u32[]{:S(2)}) collective-permute-start(bf16[2,2,9,16,256]{4,3,2,1,0:T(8,128)(2,1)S(1)} %get-tuple-element.31.chunk_ref), channel_id=1, source_target_pairs={{0,4},{1,29},{2,6},{3,31},{4,8},{5,1},{6,10},{7,3},{8,12},{9,5},{1... | collective-permute-start | bytes 884744 | tf_op jit(solution)/shard_map/ppermute | solution.py:35
  28.0 1.7 %copy-done = f32[1,1,3,3,256,256]{5,4,3,2,1,0:T(8,128)S(1)} copy-done((f32[1,1,3,3,256,256]{5,4,3,2,1,0:T(8,128)S(1)}, f32[1,1,3,3,256,256]{5,4,3,2,1,0:T(8,128)}, u32[]{:S(2)}) %copy-start) | copy-done | bytes 2359320
  29.9 2.7 %collective-permute-start.15 = (bf16[2,9,16,256]{3,2,1,0:T(8,128)(2,1)S(1)}, bf16[2,9,16,256]{3,2,1,0:T(8,128)(2,1)S(1)}, u32[]{:S(2)}, u32[]{:S(2)}) collective-permute-start(bf16[2,9,16,256]{3,2,1,0:T(8,128)(2,1)S(1)} %get-tuple-element.32), channel_id=1, source_target_pairs={{0,8},{1,25},{2,10},{3,27},{4,12},{5,29},{6,14},{7,31},{8,16},{9,1... | collective-permute-start | bytes 442376 | tf_op jit(solution)/shard_map/ppermute | solution.py:35
  33.1 2.8 %collective-permute-done.15.two_ref = bf16[2,9,16,256]{3,2,1,0:T(8,128)(2,1)S(1)} collective-permute-done((bf16[2,9,16,256]{3,2,1,0:T(8,128)(2,1)S(1)}, bf16[2,9,16,256]{3,2,1,0:T(8,128)(2,1)S(1)}, u32[]{:S(2)}, u32[]{:S(2)}) %collective-permute-start.15) | collective-permute-done | bytes 147488 | tf_op jit(solution)/shard_map/ppermute | solution.py:35
  36.0 2.7 %collective-permute-start.16 = (bf16[2,9,16,256]{3,2,1,0:T(8,128)(2,1)S(1)}, bf16[2,9,16,256]{3,2,1,0:T(8,128)(2,1)S(1)}, u32[]{:S(2)}, u32[]{:S(2)}) collective-permute-start(bf16[2,9,16,256]{3,2,1,0:T(8,128)(2,1)S(1)} %collective-permute-done.15.two_ref), channel_id=1, source_target_pairs={{0,1},{1,0},{2,3},{3,2},{4,5},{5,4},{6,7},{7,6},{8,9},{9,8},{10,11... | collective-permute-start | bytes 442376 | tf_op jit(solution)/shard_map/ppermute | solution.py:35
  40.8 2.6 %shard_map.130 = (bf16[512,256]{1,0:T(8,128)(2,1)S(1)}, bf16[576,256]{1,0:T(8,128)(2,1)S(1)}) custom-call(bf16[576,768]{1,0:T(8,128)(2,1)S(1)} %get-tuple-element.30.col_ref, f32[512,256]{1,0:T(8,128)S(1)} %bitcast.27, bf16[9,256,256]{2,1,0:T(8,128)(2,1)S(1)} %bitcast.13), custom_call_target="tpu_custom_call" | custom-call | flops 1207959552 | bytes 3145728 | tf_op jit(solution)/shard_map/pallas_call | solution.py:85
  47.2 16.0 %collective-permute-done.17.arrived_ref = bf16[512,256]{1,0:T(8,128)(2,1)S(1)} collective-permute-done((bf16[512,256]{1,0:T(8,128)(2,1)S(1)}, bf16[512,256]{1,0:T(8,128)(2,1)S(1)}, u32[]{:S(2)}, u32[]{:S(2)}) %collective-permute-start.17) | collective-permute-done | bytes 262176 | tf_op jit(solution)/shard_map/ppermute | solution.py:35
  63.3 1.5 %shard_map.133 = (f32[8,9,16,256]{3,2,1,0:T(8,128)S(1)}, bf16[8,9,16,256]{3,2,1,0:T(8,128)(2,1)S(1)}, bf16[576,256]{1,0:T(8,128)(2,1)S(1)}, f32[512,256]{1,0:T(8,128)S(1)}) custom-call(f32[64]{0:T(128)S(1)} %copy-done.6, s32[1]{0:T(128)S(6)} %copy.13.index_ref, bf16[512,256]{1,0:T(8,128)(2,1)S(1)} %collective-permute-done.17.arrived_ref, ...), custom_call_target="tpu_custom_call" | custom-call | flops 603979776 | bytes 7045380 | tf_op jit(solution)/shard_map/pallas_call | solution.py:85
  65.5 5.7 %collective-permute-start.2 = (bf16[9,16,256]{2,1,0:T(8,128)(2,1)S(1)}, bf16[9,16,256]{2,1,0:T(8,128)(2,1)S(1)}, u32[]{:S(2)}, u32[]{:S(2)}) collective-permute-start(bf16[9,16,256]{2,1,0:T(8,128)(2,1)S(1)} %shard_map.122.pair_ref), channel_id=1, source_target_pairs={{0,16},{1,19},{2,18},{3,17},{4,20},{5,23},{6,22},{7,21},{8,24},{9,... | collective-permute-start | bytes 221192 | tf_op jit(solution)/shard_map/ppermute | solution.py:35
  72.3 5.0 %collective-permute-done.2.far_ref = bf16[9,16,256]{2,1,0:T(8,128)(2,1)S(1)} collective-permute-done((bf16[9,16,256]{2,1,0:T(8,128)(2,1)S(1)}, bf16[9,16,256]{2,1,0:T(8,128)(2,1)S(1)}, u32[]{:S(2)}, u32[]{:S(2)}) %collective-permute-start.2) | collective-permute-done | bytes 73760 | tf_op jit(solution)/shard_map/ppermute | solution.py:35
  78.7 1.5 %collective-permute-start.6 = (bf16[2,9,16,256]{3,2,1,0:T(8,128)(2,1)S(1)}, bf16[2,9,16,256]{3,2,1,0:T(8,128)(2,1)S(1)}, u32[]{:S(2)}, u32[]{:S(2)}) collective-permute-start(bf16[2,9,16,256]{3,2,1,0:T(8,128)(2,1)S(1)} %get-tuple-element.29), channel_id=1, source_target_pairs={{0,8},{1,25},{2,10},{3,27},{4,12},{5,29},{6,14},{7,31},{8,16},{9,1... | collective-permute-start | bytes 442376 | tf_op jit(solution)/shard_map/ppermute | solution.py:35
  80.2 5.9 %collective-permute-done.4.one_ref = bf16[2,2,9,16,256]{4,3,2,1,0:T(8,128)(2,1)S(1)} collective-permute-done((bf16[2,2,9,16,256]{4,3,2,1,0:T(8,128)(2,1)S(1)}, bf16[2,2,9,16,256]{4,3,2,1,0:T(8,128)(2,1)S(1)}, u32[]{:S(2)}, u32[]{:S(2)}) %collective-permute-start.4) | collective-permute-done | bytes 294944 | tf_op jit(solution)/shard_map/ppermute | solution.py:35
  86.2 2.2 %collective-permute-start.5 = (bf16[2,2,9,16,256]{4,3,2,1,0:T(8,128)(2,1)S(1)}, bf16[2,2,9,16,256]{4,3,2,1,0:T(8,128)(2,1)S(1)}, u32[]{:S(2)}, u32[]{:S(2)}) collective-permute-start(bf16[2,2,9,16,256]{4,3,2,1,0:T(8,128)(2,1)S(1)} %collective-permute-done.4.one_ref), channel_id=1, source_target_pairs={{0,1},{1,0},{2,3},{3,2},{4,5},{5,4},{6,7},{7,6},{8,9},{9,8},{10,11... | collective-permute-start | bytes 884744 | tf_op jit(solution)/shard_map/ppermute | solution.py:35
  91.1 3.5 %collective-permute-start.8 = (bf16[512,256]{1,0:T(8,128)(2,1)S(1)}, bf16[512,256]{1,0:T(8,128)(2,1)S(1)}, u32[]{:S(2)}, u32[]{:S(2)}) collective-permute-start(bf16[512,256]{1,0:T(8,128)(2,1)S(1)} %shard_map.125), channel_id=1, source_target_pairs={{0,32},{1,33},{2,34},{3,35},{4,36},{5,37},{6,38},{7,39},{8,40},{9,... | collective-permute-start | bytes 786440 | tf_op jit(solution)/shard_map/ppermute | solution.py:35
  94.6 1.5 %collective-permute-done.21.one_ref = bf16[2,2,9,16,256]{4,3,2,1,0:T(8,128)(2,1)S(1)} collective-permute-done((bf16[2,2,9,16,256]{4,3,2,1,0:T(8,128)(2,1)S(1)}, bf16[2,2,9,16,256]{4,3,2,1,0:T(8,128)(2,1)S(1)}, u32[]{:S(2)}, u32[]{:S(2)}) %collective-permute-start.21) | collective-permute-done | bytes 294944 | tf_op jit(solution)/shard_map/ppermute | solution.py:35
  96.2 2.2 %collective-permute-start.23 = (bf16[2,9,16,256]{3,2,1,0:T(8,128)(2,1)S(1)}, bf16[2,9,16,256]{3,2,1,0:T(8,128)(2,1)S(1)}, u32[]{:S(2)}, u32[]{:S(2)}) collective-permute-start(bf16[2,9,16,256]{3,2,1,0:T(8,128)(2,1)S(1)} %get-tuple-element.48), channel_id=1, source_target_pairs={{0,1},{1,0},{2,3},{3,2},{4,5},{5,4},{6,7},{7,6},{8,9},{9,8},{10,11... | collective-permute-start | bytes 442376 | tf_op jit(solution)/shard_map/ppermute | solution.py:35
  99.4 6.4 %collective-permute-start.24 = (bf16[9,16,256]{2,1,0:T(8,128)(2,1)S(1)}, bf16[9,16,256]{2,1,0:T(8,128)(2,1)S(1)}, u32[]{:S(2)}, u32[]{:S(2)}) collective-permute-start(bf16[9,16,256]{2,1,0:T(8,128)(2,1)S(1)} %get-tuple-element.49), channel_id=1, source_target_pairs={{0,224},{1,242},{2,225},{3,243},{4,228},{5,246},{6,229},{7,247},{8... | collective-permute-start | bytes 221192 | tf_op jit(solution)/shard_map/ppermute | solution.py:35
  105.8 1.6 %shard_map.134 = f32[512,256]{1,0:T(8,128)} custom-call(f32[512,256]{1,0:T(8,128)S(1)} %get-tuple-element.38.cot_ref, bf16[576,256]{1,0:T(8,128)(2,1)S(1)} %get-tuple-element.39.dpad_ref, bf16[9,256,256]{2,1,0:T(8,128)(2,1)S(1)} %bitcast.15), custom_call_target="tpu_custom_call" | custom-call | flops 603979776 | bytes 2523136 | tf_op jit(solution)/shard_map/pallas_call | solution.py:85
  108.5 9.6 %collective-permute-done.25.b_ref = bf16[9,16,256]{2,1,0:T(8,128)(2,1)S(1)} collective-permute-done((bf16[9,16,256]{2,1,0:T(8,128)(2,1)S(1)}, bf16[9,16,256]{2,1,0:T(8,128)(2,1)S(1)}, u32[]{:S(2)}, u32[]{:S(2)}) %collective-permute-start.25) | collective-permute-done | bytes 73760 | tf_op jit(solution)/shard_map/ppermute | solution.py:35
  118.3 1.6 %shard_map.126 = f32[512,256]{1,0:T(8,128)} custom-call(bf16[512,256]{1,0:T(8,128)(2,1)S(1)} %collective-permute-done.8.arrived_ref, f32[512,256]{1,0:T(8,128)S(1)} %bitcast.23, bf16[9,256,256]{2,1,0:T(8,128)(2,1)S(1)} %bitcast.17), custom_call_target="tpu_custom_call" | custom-call | flops 603979776 | bytes 2490368 | tf_op jit(solution)/shard_map/pallas_call | solution.py:85
  (71 shorter events, 17.9 us)
Async XLA Ops:
  1.5 4.1 %collective-permute-start = (bf16[9,8,256]{2,1,0:T(8,128)(2,1)S(1)}, bf16[9,8,256]{2,1,0:T(8,128)(2,1)S(1)}, u32[]{:S(2)}, u32[]{:S(2)}) collective-permute-start(bf16[9,8,256]{2,1,0:T(8,128)(2,1)S(1)} %bitcast.24), channel_id=1, source_target_pairs={{0,1},{1,0},{2,3},{3,2},{4,5},{5,4},{6,7},{7,6},{8,9},{9,8},{10,11... | collective-permute-start | bytes 110600 | tf_op jit(solution)/shard_map/ppermute | solution.py:35
  5.6 10.0 %collective-permute-start.9 = (bf16[9,16,256]{2,1,0:T(8,128)(2,1)S(1)}, bf16[9,16,256]{2,1,0:T(8,128)(2,1)S(1)}, u32[]{:S(2)}, u32[]{:S(2)}) collective-permute-start(bf16[9,16,256]{2,1,0:T(8,128)(2,1)S(1)} %shard_map.122.pair_ref), channel_id=1, source_target_pairs={{0,224},{1,227},{2,226},{3,225},{4,228},{5,231},{6,230},{7,229},{8... | collective-permute-start | bytes 221192 | tf_op jit(solution)/shard_map/ppermute | solution.py:35
  8.9 12.1 %collective-permute-start.11 = (bf16[9,16,256]{2,1,0:T(8,128)(2,1)S(1)}, bf16[9,16,256]{2,1,0:T(8,128)(2,1)S(1)}, u32[]{:S(2)}, u32[]{:S(2)}) collective-permute-start(bf16[9,16,256]{2,1,0:T(8,128)(2,1)S(1)} %shard_map.122.pair_ref), channel_id=1, source_target_pairs={{0,240},{1,243},{2,242},{3,241},{4,244},{5,247},{6,246},{7,245},{8... | collective-permute-start | bytes 221192 | tf_op jit(solution)/shard_map/ppermute | solution.py:35
  15.6 5.3 %collective-permute-start.10 = (bf16[9,16,256]{2,1,0:T(8,128)(2,1)S(1)}, bf16[9,16,256]{2,1,0:T(8,128)(2,1)S(1)}, u32[]{:S(2)}, u32[]{:S(2)}) collective-permute-start(bf16[9,16,256]{2,1,0:T(8,128)(2,1)S(1)} %collective-permute-done.9.near_ref), channel_id=1, source_target_pairs={{0,1},{1,0},{2,3},{3,2},{4,5},{5,4},{6,7},{7,6},{8,9},{9,8},{10,11... | collective-permute-start | bytes 221192 | tf_op jit(solution)/shard_map/ppermute | solution.py:35
  22.3 10.3 %collective-permute-start.13 = (bf16[2,2,9,16,256]{4,3,2,1,0:T(8,128)(2,1)S(1)}, bf16[2,2,9,16,256]{4,3,2,1,0:T(8,128)(2,1)S(1)}, u32[]{:S(2)}, u32[]{:S(2)}) collective-permute-start(bf16[2,2,9,16,256]{4,3,2,1,0:T(8,128)(2,1)S(1)} %get-tuple-element.31.chunk_ref), channel_id=1, source_target_pairs={{0,4},{1,29},{2,6},{3,31},{4,8},{5,1},{6,10},{7,3},{8,12},{9,5},{1... | collective-permute-start | bytes 884744 | tf_op jit(solution)/shard_map/ppermute | solution.py:35
  29.8 15.6 %collective-permute-start.19 = (bf16[8,9,16,256]{3,2,1,0:T(8,128)(2,1)S(1)}, bf16[8,9,16,256]{3,2,1,0:T(8,128)(2,1)S(1)}, u32[]{:S(2)}, u32[]{:S(2)}) collective-permute-start(bf16[8,9,16,256]{3,2,1,0:T(8,128)(2,1)S(1)} %get-tuple-element.43), channel_id=1, source_target_pairs={{0,1},{1,0},{2,3},{3,2},{4,5},{5,4},{6,7},{7,6},{8,9},{9,8},{10,11... | collective-permute-start | bytes 1769480 | tf_op jit(solution)/shard_map/ppermute | solution.py:35
  29.9 6.1 %collective-permute-start.15 = (bf16[2,9,16,256]{3,2,1,0:T(8,128)(2,1)S(1)}, bf16[2,9,16,256]{3,2,1,0:T(8,128)(2,1)S(1)}, u32[]{:S(2)}, u32[]{:S(2)}) collective-permute-start(bf16[2,9,16,256]{3,2,1,0:T(8,128)(2,1)S(1)} %get-tuple-element.32), channel_id=1, source_target_pairs={{0,8},{1,25},{2,10},{3,27},{4,12},{5,29},{6,14},{7,31},{8,16},{9,1... | collective-permute-start | bytes 442376 | tf_op jit(solution)/shard_map/ppermute | solution.py:35
  32.6 7.2 %collective-permute-start.14 = (bf16[2,2,9,16,256]{4,3,2,1,0:T(8,128)(2,1)S(1)}, bf16[2,2,9,16,256]{4,3,2,1,0:T(8,128)(2,1)S(1)}, u32[]{:S(2)}, u32[]{:S(2)}) collective-permute-start(bf16[2,2,9,16,256]{4,3,2,1,0:T(8,128)(2,1)S(1)} %collective-permute-done.13.one_ref), channel_id=1, source_target_pairs={{0,1},{1,0},{2,3},{3,2},{4,5},{5,4},{6,7},{7,6},{8,9},{9,8},{10,11... | collective-permute-start | bytes 884744 | tf_op jit(solution)/shard_map/ppermute | solution.py:35
  36.0 3.8 %collective-permute-start.16 = (bf16[2,9,16,256]{3,2,1,0:T(8,128)(2,1)S(1)}, bf16[2,9,16,256]{3,2,1,0:T(8,128)(2,1)S(1)}, u32[]{:S(2)}, u32[]{:S(2)}) collective-permute-start(bf16[2,9,16,256]{3,2,1,0:T(8,128)(2,1)S(1)} %collective-permute-done.15.two_ref), channel_id=1, source_target_pairs={{0,1},{1,0},{2,3},{3,2},{4,5},{5,4},{6,7},{7,6},{8,9},{9,8},{10,11... | collective-permute-start | bytes 442376 | tf_op jit(solution)/shard_map/ppermute | solution.py:35
  43.4 19.8 %collective-permute-start.17 = (bf16[512,256]{1,0:T(8,128)(2,1)S(1)}, bf16[512,256]{1,0:T(8,128)(2,1)S(1)}, u32[]{:S(2)}, u32[]{:S(2)}) collective-permute-start(bf16[512,256]{1,0:T(8,128)(2,1)S(1)} %get-tuple-element.33), channel_id=1, source_target_pairs={{0,32},{1,33},{2,34},{3,35},{4,36},{5,37},{6,38},{7,39},{8,40},{9,... | collective-permute-start | bytes 786440 | tf_op jit(solution)/shard_map/ppermute | solution.py:35
  45.5 42.9 %collective-permute-start.20 = (bf16[8,9,16,256]{3,2,1,0:T(8,128)(2,1)S(1)}, bf16[8,9,16,256]{3,2,1,0:T(8,128)(2,1)S(1)}, u32[]{:S(2)}, u32[]{:S(2)}) collective-permute-start(bf16[8,9,16,256]{3,2,1,0:T(8,128)(2,1)S(1)} %shard_map.136), channel_id=1, source_target_pairs={{0,224},{1,225},{2,226},{3,227},{4,228},{5,229},{6,230},{7,231},{8... | collective-permute-start | bytes 1769480 | tf_op jit(solution)/shard_map/ppermute | solution.py:35
  64.8 23.6 %collective-permute-start.18 = (bf16[8,9,16,256]{3,2,1,0:T(8,128)(2,1)S(1)}, bf16[8,9,16,256]{3,2,1,0:T(8,128)(2,1)S(1)}, u32[]{:S(2)}, u32[]{:S(2)}) collective-permute-start(bf16[8,9,16,256]{3,2,1,0:T(8,128)(2,1)S(1)} %get-tuple-element.41), channel_id=1, source_target_pairs={{0,1},{1,0},{2,3},{3,2},{4,5},{5,4},{6,7},{7,6},{8,9},{9,8},{10,11... | collective-permute-start | bytes 1769480 | tf_op jit(solution)/shard_map/ppermute | solution.py:35
  65.5 11.8 %collective-permute-start.2 = (bf16[9,16,256]{2,1,0:T(8,128)(2,1)S(1)}, bf16[9,16,256]{2,1,0:T(8,128)(2,1)S(1)}, u32[]{:S(2)}, u32[]{:S(2)}) collective-permute-start(bf16[9,16,256]{2,1,0:T(8,128)(2,1)S(1)} %shard_map.122.pair_ref), channel_id=1, source_target_pairs={{0,16},{1,19},{2,18},{3,17},{4,20},{5,23},{6,22},{7,21},{8,24},{9,... | collective-permute-start | bytes 221192 | tf_op jit(solution)/shard_map/ppermute | solution.py:35
  71.2 6.1 %collective-permute-start.1 = (bf16[9,16,256]{2,1,0:T(8,128)(2,1)S(1)}, bf16[9,16,256]{2,1,0:T(8,128)(2,1)S(1)}, u32[]{:S(2)}, u32[]{:S(2)}) collective-permute-start(bf16[9,16,256]{2,1,0:T(8,128)(2,1)S(1)} %shard_map.122.pair_ref), channel_id=1, source_target_pairs={{0,2},{1,3},{2,0},{3,1},{4,6},{5,7},{6,4},{7,5},{8,10},{9,11},{10,... | collective-permute-start | bytes 221192 | tf_op jit(solution)/shard_map/ppermute | solution.py:35
  78.6 7.5 %collective-permute-start.4 = (bf16[2,2,9,16,256]{4,3,2,1,0:T(8,128)(2,1)S(1)}, bf16[2,2,9,16,256]{4,3,2,1,0:T(8,128)(2,1)S(1)}, u32[]{:S(2)}, u32[]{:S(2)}) collective-permute-start(bf16[2,2,9,16,256]{4,3,2,1,0:T(8,128)(2,1)S(1)} %get-tuple-element.28.chunk_ref), channel_id=1, source_target_pairs={{0,4},{1,29},{2,6},{3,31},{4,8},{5,1},{6,10},{7,3},{8,12},{9,5},{1... | collective-permute-start | bytes 884744 | tf_op jit(solution)/shard_map/ppermute | solution.py:35
  78.7 10.0 %collective-permute-start.6 = (bf16[2,9,16,256]{3,2,1,0:T(8,128)(2,1)S(1)}, bf16[2,9,16,256]{3,2,1,0:T(8,128)(2,1)S(1)}, u32[]{:S(2)}, u32[]{:S(2)}) collective-permute-start(bf16[2,9,16,256]{3,2,1,0:T(8,128)(2,1)S(1)} %get-tuple-element.29), channel_id=1, source_target_pairs={{0,8},{1,25},{2,10},{3,27},{4,12},{5,29},{6,14},{7,31},{8,16},{9,1... | collective-permute-start | bytes 442376 | tf_op jit(solution)/shard_map/ppermute | solution.py:35
  86.2 4.0 %collective-permute-start.5 = (bf16[2,2,9,16,256]{4,3,2,1,0:T(8,128)(2,1)S(1)}, bf16[2,2,9,16,256]{4,3,2,1,0:T(8,128)(2,1)S(1)}, u32[]{:S(2)}, u32[]{:S(2)}) collective-permute-start(bf16[2,2,9,16,256]{4,3,2,1,0:T(8,128)(2,1)S(1)} %collective-permute-done.4.one_ref), channel_id=1, source_target_pairs={{0,1},{1,0},{2,3},{3,2},{4,5},{5,4},{6,7},{7,6},{8,9},{9,8},{10,11... | collective-permute-start | bytes 884744 | tf_op jit(solution)/shard_map/ppermute | solution.py:35
  88.6 7.5 %collective-permute-start.21 = (bf16[2,2,9,16,256]{4,3,2,1,0:T(8,128)(2,1)S(1)}, bf16[2,2,9,16,256]{4,3,2,1,0:T(8,128)(2,1)S(1)}, u32[]{:S(2)}, u32[]{:S(2)}) collective-permute-start(bf16[2,2,9,16,256]{4,3,2,1,0:T(8,128)(2,1)S(1)} %get-tuple-element.44), channel_id=1, source_target_pairs={{0,4},{1,29},{2,6},{3,31},{4,8},{5,1},{6,10},{7,3},{8,12},{9,5},{1... | collective-permute-start | bytes 884744 | tf_op jit(solution)/shard_map/ppermute | solution.py:35
  88.8 5.8 %collective-permute-start.22 = (bf16[2,9,16,256]{3,2,1,0:T(8,128)(2,1)S(1)}, bf16[2,9,16,256]{3,2,1,0:T(8,128)(2,1)S(1)}, u32[]{:S(2)}, u32[]{:S(2)}) collective-permute-start(bf16[2,9,16,256]{3,2,1,0:T(8,128)(2,1)S(1)} %get-tuple-element.45), channel_id=1, source_target_pairs={{0,8},{1,25},{2,10},{3,27},{4,12},{5,29},{6,14},{7,31},{8,16},{9,1... | collective-permute-start | bytes 442376 | tf_op jit(solution)/shard_map/ppermute | solution.py:35
  91.1 27.2 %collective-permute-start.8 = (bf16[512,256]{1,0:T(8,128)(2,1)S(1)}, bf16[512,256]{1,0:T(8,128)(2,1)S(1)}, u32[]{:S(2)}, u32[]{:S(2)}) collective-permute-start(bf16[512,256]{1,0:T(8,128)(2,1)S(1)} %shard_map.125), channel_id=1, source_target_pairs={{0,32},{1,33},{2,34},{3,35},{4,36},{5,37},{6,38},{7,39},{8,40},{9,... | collective-permute-start | bytes 786440 | tf_op jit(solution)/shard_map/ppermute | solution.py:35
  96.2 3.2 %collective-permute-start.23 = (bf16[2,9,16,256]{3,2,1,0:T(8,128)(2,1)S(1)}, bf16[2,9,16,256]{3,2,1,0:T(8,128)(2,1)S(1)}, u32[]{:S(2)}, u32[]{:S(2)}) collective-permute-start(bf16[2,9,16,256]{3,2,1,0:T(8,128)(2,1)S(1)} %get-tuple-element.48), channel_id=1, source_target_pairs={{0,1},{1,0},{2,3},{3,2},{4,5},{5,4},{6,7},{7,6},{8,9},{9,8},{10,11... | collective-permute-start | bytes 442376 | tf_op jit(solution)/shard_map/ppermute | solution.py:35
  99.4 9.1 %collective-permute-start.24 = (bf16[9,16,256]{2,1,0:T(8,128)(2,1)S(1)}, bf16[9,16,256]{2,1,0:T(8,128)(2,1)S(1)}, u32[]{:S(2)}, u32[]{:S(2)}) collective-permute-start(bf16[9,16,256]{2,1,0:T(8,128)(2,1)S(1)} %get-tuple-element.49), channel_id=1, source_target_pairs={{0,224},{1,242},{2,225},{3,243},{4,228},{5,246},{6,229},{7,247},{8... | collective-permute-start | bytes 221192 | tf_op jit(solution)/shard_map/ppermute | solution.py:35
  105.8 12.3 %collective-permute-start.25 = (bf16[9,16,256]{2,1,0:T(8,128)(2,1)S(1)}, bf16[9,16,256]{2,1,0:T(8,128)(2,1)S(1)}, u32[]{:S(2)}, u32[]{:S(2)}) collective-permute-start(bf16[9,16,256]{2,1,0:T(8,128)(2,1)S(1)} %get-tuple-element.50), channel_id=1, source_target_pairs={{0,240},{1,226},{2,241},{3,227},{4,244},{5,230},{6,245},{7,231},{8... | collective-permute-start | bytes 221192 | tf_op jit(solution)/shard_map/ppermute | solution.py:35
  118.1 1.7 %collective-permute-start.26 = (bf16[9,8,256]{2,1,0:T(8,128)(2,1)S(1)}, bf16[9,8,256]{2,1,0:T(8,128)(2,1)S(1)}, u32[]{:S(2)}, u32[]{:S(2)}) collective-permute-start(bf16[9,8,256]{2,1,0:T(8,128)(2,1)S(1)} %get-tuple-element.52), channel_id=1, source_target_pairs={{0,1},{1,0},{2,3},{3,2},{4,5},{5,4},{6,7},{7,6},{8,9},{9,8},{10,11... | collective-permute-start | bytes 110600 | tf_op jit(solution)/shard_map/ppermute | solution.py:35
  (12 other events, 73.5 us)
where the time goes:
time: 121 us
  waiting for transfers between devices  52.3 us (43%)
  starting transfers between devices  50.7 us (42%)
  Pallas kernels  11.8 us (10%)
  local copies, waits for them, and re-layouts  2.61 us (2%)
  between operations  1.56 us (1%)
  other arithmetic  1.55 us (1%)
    ppermute x27, waiting for transfers between devices, moved(): return lax.ppermute(value, ('pipe', 'dp'), pairs)  52.3 us
    ppermute x27, starting transfers between devices, moved(): return lax.ppermute(value, ('pipe', 'dp'), pairs)  50.7 us
    pallas_call x20, Pallas kernels, call(): pl.pallas_call(kernel, out_shape=outs, in_specs=specs + [pl.BlockSpec(mem...  11.8 us
    unnamed x18, local copies, waits for them, and re-layouts  2.61 us
  transfers between devices with their start and end apart: 27, of which 13 were waited for; matrix products, arithmetic and copies ran while one was open for 0% of the time, Pallas kernels for 10%

commit v1 on v0

--- a/solution.py
+++ b/solution.py
@@ -1,3 +1,5 @@
+import functools
+
 import jax
 import jax.numpy as jnp
 from jax import lax
@@ -47,15 +49,16 @@
     return moved(value, lambda p, z, y, c: (PIPE - 1 - p, z, y, c))
 
 
-def to_plane(value, flip, far):
-    def where(p, z, y, c):
-        return (PIPE - 1 - p if flip else p, z + 4 * far, y ^ c, c)
-
-    return moved(value, where)
-
-
-def to_owner(value, far):
-    return moved(value, lambda p, z, y, c: (PIPE - 1 - p, z + 4 * (c ^ far), c, y))
+def to_plane(value):
+    return moved(value, lambda p, z, y, c: (PIPE - 1 - p, z, y ^ c, c))
+
+
+def to_owner(value):
+    return moved(value, lambda p, z, y, c: (PIPE - 1 - p, z, c, y))
+
+
+def to_far(value):
+    return moved(value, lambda p, z, y, c: (p, z + 4, y, c))
 
 
 def to_next(value):
@@ -146,32 +149,21 @@
             store(3 * a + b, (g[b * C : (b + 1) * C] * SCALE).reshape(Z * Y, 16, C))
 
 
-def pair_kernel(own_ref, other_ref, pair_ref):
+def pair_kernel(own_ref, other_ref, far_ref, far_other_ref, pair_ref):
     _, _, core = place()
-    mine, theirs = own_ref[...].astype(f32), other_ref[...].astype(f32)
-    low, high = jnp.where(core == 0, mine, theirs), jnp.where(core == 0, theirs, mine)
-    pair_ref[...] = jnp.concatenate([low, high], axis=1).astype(bf16)
-
-
-def fill_plane(chunk_ref, half_ref, near, far):
+    for dz, mine, theirs in ((0, own_ref, other_ref), (1, far_ref, far_other_ref)):
+        m, t = mine[...].astype(f32), theirs[...].astype(f32)
+        low, high = jnp.where(core == 0, m, t), jnp.where(core == 0, t, m)
+        pair_ref[dz] = jnp.concatenate([low, high], axis=1).astype(bf16)
+
+
+def plane_kernel(split, first_ref, second_ref, chunk_ref, half_ref):
     _, y, core = place()
-    half = y ^ core
-    chunk_ref[0, near[0]] = near[1][...]
-    chunk_ref[0, 1 - near[0]] = near[2][...]
-    chunk_ref[1, half] = far[0][...]
-    chunk_ref[1, 1 - half] = far[1][...]
-    for dz in range(2):
+    half = y ^ core if split else y
+    for dz in range(2):
+        chunk_ref[dz, half] = first_ref[dz]
+        chunk_ref[dz, 1 - half] = second_ref[dz]
         half_ref[dz] = chunk_ref[dz, core]
-
-
-def plane_mirror_kernel(near_ref, near_core_ref, far_ref, far_core_ref, chunk_ref, half_ref):
-    _, y, core = place()
-    fill_plane(chunk_ref, half_ref, (y ^ core, near_ref, near_core_ref), (far_ref, far_core_ref))
-
-
-def plane_own_kernel(pair_ref, other_ref, far_ref, far_core_ref, chunk_ref, half_ref):
-    _, y, _ = place()
-    fill_plane(chunk_ref, half_ref, (y, pair_ref, other_ref), (far_ref, far_core_ref))
 
 
 def assemble_kernel(chunk_ref, one_ref, one_core_ref, two_ref, two_core_ref, w_ref):
@@ -280,13 +272,9 @@
     share_out(acc_ref, keep_ref, send_ref)
 
 
-def earlier_sum_kernel(keep_ref, got_ref, out_ref):
-    out_ref[...] = (keep_ref[...] + got_ref[...].astype(f32)).astype(bf16)
-
-
-def core_sum_kernel(keep_ref, got_ref, earlier_ref, one_ref, two_ref, mine_ref):
+def core_sum_kernel(keep_ref, got_ref, one_ref, two_ref, mine_ref):
     def total(j):
-        return keep_ref[j] + got_ref[j].astype(f32) + earlier_ref[j].astype(f32)
+        return keep_ref[j] + got_ref[j].astype(f32)
 
     for dz in range(2):
         for half in range(Y):
@@ -302,18 +290,24 @@
         send_ref[dz] = one_ref[dz, 1 - core]
 
 
-def z_core_sum_kernel(keep_ref, got_ref, near_ref, far_ref):
+def add_kernel(keep_ref, *refs):
+    total = keep_ref[...]
+    for ref in refs[:-1]:
+        total = total + ref[...].astype(f32)
+    refs[-1][...] = total.astype(bf16)
+
+
+def last_split_kernel(got_ref, keep_ref, send_ref, total_ref):
     _, _, core = place()
-    for dz, out_ref in ((core, near_ref), (1 - core, far_ref)):
-        out_ref[...] = (keep_ref[dz] + got_ref[dz].astype(f32)).astype(bf16)
-
-
-def last_sum_kernel(a_ref, b_ref, keep_ref, send_ref, total_ref):
-    _, _, core = place()
-    total = a_ref[...].astype(f32) + b_ref[...].astype(f32)
-    total_ref[...] = total.reshape(TAPS, CORES, 8, C)
-    keep_ref[...] = total_ref[:, core]
-    send_ref[...] = total_ref[:, 1 - core].astype(bf16)
+    for dz in range(2):
+        total_ref[...] = got_ref[dz].astype(f32).reshape(TAPS, CORES, 8, C)
+        keep_ref[dz] = total_ref[:, core]
+        send_ref[dz] = total_ref[:, 1 - core].astype(bf16)
+
+
+def last_sum_kernel(keep_ref, got_ref, near_ref, far_ref):
+    near_ref[...] = keep_ref[0] + got_ref[0].astype(f32)
+    far_ref[...] = (keep_ref[1] + got_ref[1].astype(f32)).astype(bf16)
 
 
 CONV_FLOPS = 2 * PIX * TAPS * C * C
@@ -325,7 +319,7 @@
 TOTAL = shape((TAPS, Z * Y, 16, C), f32)
 CHUNK = shape((2, Y, TAPS, 16, C), bf16)
 HALF = shape((2, TAPS, 16, C), bf16)
-PAIR = shape((TAPS, 16, C), bf16)
+HALF32 = shape(HALF.shape, f32)
 
 
 def assembled(chunk, half):
@@ -335,19 +329,25 @@
     return w.reshape(TAPS, C, C)
 
 
+def summed(keep, send):
+    one, two, mine = call(core_sum_kernel, [CHUNK, HALF, HALF32], [keep, to_core(send)])
+    got = [to_z(one, 1), to_z(two, 2)]
+    keep, send = call(z_sum_kernel, [HALF32, HALF], got + [mine])
+    return [keep, to_core(send)]
+
+
 def body(
     master, grad_acc, down_act, down_next, up_stash, up_order, up_grad, up_next, ex_table, ex_index
 ):
     own = master.reshape(TAPS, 8, C).astype(bf16)
-    pair = call(pair_kernel, [PAIR], [own, to_core(own)])[0]
-
-    far = to_plane(pair, True, 1)
-    near = to_plane(pair, True, 0)
-    chunk, half = call(plane_mirror_kernel, [CHUNK, HALF], [near, to_core(near), far, to_core(far)])
+    far = to_far(own)
+    pair = call(pair_kernel, [HALF], [own, to_core(own), far, to_core(far)])[0]
+
+    got = to_plane(pair)
+    chunk, half = call(functools.partial(plane_kernel, True), [CHUNK, HALF], [got, to_core(got)])
     w_mirror = assembled(chunk, half)
 
     own_other = to_y(pair)
-    own_far = to_plane(pair, False, 1)
     act = down_act.reshape(PIX, C)
     stash = up_stash.reshape(2, PIX, C)
     col1, xt1, col2, xt2 = call(
@@ -357,8 +357,9 @@
 
     lists = [shape((8, TAPS, 16, C), f32), shape((8, TAPS, 16, C), bf16)]
     keep_e, send_e = call(earlier_kernel, lists, [grad_acc.reshape(TAPS, Z * Y, 16, C)])
-    earlier = call(earlier_sum_kernel, lists[1:], [keep_e, to_core(send_e)])[0]
-    earlier_moved = to_mirror(earlier)
+    earlier = summed(keep_e, send_e)
+    earlier = call(add_kernel, [HALF], earlier)[0]
+    earlier = to_mirror(earlier)
 
     back, dpad1 = call(
         up_first_kernel,
@@ -369,7 +370,7 @@
     )
     passed = to_next(back)
     own_chunk, own_half = call(
-        plane_own_kernel, [CHUNK, HALF], [pair, own_other, own_far, to_core(own_far)]
+        functools.partial(plane_kernel, False), [CHUNK, HALF], [pair, own_other]
     )
     slope = call(slope_kernel, [FIELD], [col2, w_mirror], flops=CONV_FLOPS)[0]
     g1 = call(grad_first_kernel, [TOTAL], [xt1, dpad1], flops=CONV_FLOPS)[0]
@@ -383,10 +384,7 @@
         flops=CONV_FLOPS,
     )
 
-    one, two, mine = call(
-        core_sum_kernel, [CHUNK, HALF, shape(HALF.shape, f32)], [keep, to_core(send), earlier_moved]
-    )
-    got = [to_z(one, 1), to_z(two, 2)]
+    total = summed(keep, send)
 
     w_own = assembled(own_chunk, own_half)
     section_out = call(forward_first_kernel, [FIELD16], [col_down, act, w_own], flops=CONV_FLOPS)[0]
@@ -402,16 +400,18 @@
         flops=CONV_FLOPS,
     )[0]
 
-    keep_z, send_z = call(z_sum_kernel, [shape(HALF.shape, f32), HALF], got + [mine])
-    first, second = call(z_core_sum_kernel, [PAIR] * 2, [keep_z, to_core(send_z)])
+    total = call(add_kernel, [HALF], [*total, earlier])[0]
+    parts = [shape((2, TAPS, 8, C), f32), shape((2, TAPS, 8, C), bf16)]
     keep_l, send_l = call(
+        last_split_kernel, parts, [to_owner(total)], scratch=[pltpu.VMEM((TAPS, CORES, 8, C), f32)]
+    )
+    near_l, far_l = call(
         last_sum_kernel,
         [shape((TAPS, 8, C), f32), shape((TAPS, 8, C), bf16)],
-        [to_owner(first, 0), to_owner(second, 1)],
-        scratch=[pltpu.VMEM((TAPS, CORES, 8, C), f32)],
-    )
-    got_l = to_core(send_l)
-    total_grad = keep_l + got_l.astype(f32)
+        [keep_l, to_core(send_l)],
+    )
+    got_l = to_far(far_l)
+    total_grad = near_l + got_l.astype(f32)
     new_master = master - learning_rate * total_grad.reshape(master.shape)
     field = (1, 1, HT, WD, C)
     return (down_out.reshape(field), up_out.reshape(field), new_master)

time: 121 us -> 113 us (0.934)
  the two profiles are of different devices: /device:TPU:1 before, /device:TPU:36 now
where the time goes in v1:
time: 113 us
  waiting for transfers between devices  56.9 us (50%)
  starting transfers between devices  38.3 us (34%)
  Pallas kernels  11.9 us (11%)
  local copies, waits for them, and re-layouts  2.82 us (2%)
  between operations  1.61 us (1%)
  other arithmetic  1.55 us (1%)
    ppermute x28, waiting for transfers between devices, moved(): return lax.ppermute(value, ('pipe', 'dp'), pairs)  56.9 us
    ppermute x28, starting transfers between devices, moved(): return lax.ppermute(value, ('pipe', 'dp'), pairs)  38.3 us
    pallas_call x23, Pallas kernels, call(): pl.pallas_call(kernel, out_shape=outs, in_specs=specs + [pl.BlockSpec(mem...  11.9 us
    unnamed x18, local copies, waits for them, and re-layouts  2.82 us
  transfers between devices with their start and end apart: 28, of which 14 were waited for; matrix products, arithmetic and copies ran while one was open for 0% of the time, Pallas kernels for 8%

profile of v1, /device:TPU:36, one launch (start us, length us, event | category | flops | bytes accessed | tf_op | source)
XLA Modules:
  0.0 113.1 jit_solution(16221567439255148856)
XLA Ops:
  1.5 6.3 %collective-permute-start.1 = (bf16[9,8,256]{2,1,0:T(8,128)(2,1)S(1)}, bf16[9,8,256]{2,1,0:T(8,128)(2,1)S(1)}, u32[]{:S(2)}, u32[]{:S(2)}) collective-permute-start(bf16[9,8,256]{2,1,0:T(8,128)(2,1)S(1)} %bitcast.24), channel_id=1, source_target_pairs={{0,16},{1,17},{2,18},{3,19},{4,20},{5,21},{6,22},{7,23},{8,24},{9,... | collective-permute-start | bytes 110600 | tf_op jit(solution)/shard_map/ppermute | solution.py:37
  7.8 1.9 %collective-permute-done.1.far_ref = bf16[9,8,256]{2,1,0:T(8,128)(2,1)S(1)} collective-permute-done((bf16[9,8,256]{2,1,0:T(8,128)(2,1)S(1)}, bf16[9,8,256]{2,1,0:T(8,128)(2,1)S(1)}, u32[]{:S(2)}, u32[]{:S(2)}) %collective-permute-start.1) | collective-permute-done | bytes 36896 | tf_op jit(solution)/shard_map/ppermute | solution.py:37
  11.0 1.6 %collective-permute-start.9 = (bf16[2,9,16,256]{3,2,1,0:T(8,128)(2,1)S(1)}, bf16[2,9,16,256]{3,2,1,0:T(8,128)(2,1)S(1)}, u32[]{:S(2)}, u32[]{:S(2)}) collective-permute-start(bf16[2,9,16,256]{3,2,1,0:T(8,128)(2,1)S(1)} %shard_map.122.first_ref), channel_id=1, source_target_pairs={{0,224},{1,227},{2,226},{3,225},{4,228},{5,231},{6,230},{7,229},{8... | collective-permute-start | bytes 442376 | tf_op jit(solution)/shard_map/ppermute | solution.py:37
  12.6 5.8 %collective-permute-done.9.first_ref = bf16[2,9,16,256]{3,2,1,0:T(8,128)(2,1)S(1)} collective-permute-done((bf16[2,9,16,256]{3,2,1,0:T(8,128)(2,1)S(1)}, bf16[2,9,16,256]{3,2,1,0:T(8,128)(2,1)S(1)}, u32[]{:S(2)}, u32[]{:S(2)}) %collective-permute-start.9) | collective-permute-done | bytes 147488 | tf_op jit(solution)/shard_map/ppermute | solution.py:37
  19.8 1.7 %collective-permute-start.11 = (bf16[2,2,9,16,256]{4,3,2,1,0:T(8,128)(2,1)S(1)}, bf16[2,2,9,16,256]{4,3,2,1,0:T(8,128)(2,1)S(1)}, u32[]{:S(2)}, u32[]{:S(2)}) collective-permute-start(bf16[2,2,9,16,256]{4,3,2,1,0:T(8,128)(2,1)S(1)} %get-tuple-element.36.chunk_ref), channel_id=1, source_target_pairs={{0,4},{1,29},{2,6},{3,31},{4,8},{5,1},{6,10},{7,3},{8,12},{9,5},{1... | collective-permute-start | bytes 884744 | tf_op jit(solution)/shard_map/ppermute | solution.py:37
  21.6 4.4 %collective-permute-start.13 = (bf16[2,9,16,256]{3,2,1,0:T(8,128)(2,1)S(1)}, bf16[2,9,16,256]{3,2,1,0:T(8,128)(2,1)S(1)}, u32[]{:S(2)}, u32[]{:S(2)}) collective-permute-start(bf16[2,9,16,256]{3,2,1,0:T(8,128)(2,1)S(1)} %get-tuple-element.37), channel_id=1, source_target_pairs={{0,8},{1,25},{2,10},{3,27},{4,12},{5,29},{6,14},{7,31},{8,16},{9,1... | collective-permute-start | bytes 442376 | tf_op jit(solution)/shard_map/ppermute | solution.py:37
  26.6 5.3 %collective-permute-done.13.two_ref = bf16[2,9,16,256]{3,2,1,0:T(8,128)(2,1)S(1)} collective-permute-done((bf16[2,9,16,256]{3,2,1,0:T(8,128)(2,1)S(1)}, bf16[2,9,16,256]{3,2,1,0:T(8,128)(2,1)S(1)}, u32[]{:S(2)}, u32[]{:S(2)}) %collective-permute-start.13) | collective-permute-done | bytes 147488 | tf_op jit(solution)/shard_map/ppermute | solution.py:37
  36.0 2.6 %shard_map.130 = (bf16[512,256]{1,0:T(8,128)(2,1)S(1)}, bf16[576,256]{1,0:T(8,128)(2,1)S(1)}) custom-call(bf16[576,768]{1,0:T(8,128)(2,1)S(1)} %get-tuple-element.35.col_ref, f32[512,256]{1,0:T(8,128)S(1)} %bitcast.28, bf16[9,256,256]{2,1,0:T(8,128)(2,1)S(1)} %bitcast.13), custom_call_target="tpu_custom_call" | custom-call | flops 1207959552 | bytes 3145728 | tf_op jit(solution)/shard_map/pallas_call | solution.py:88
  38.6 3.2 %collective-permute-start.15 = (bf16[512,256]{1,0:T(8,128)(2,1)S(1)}, bf16[512,256]{1,0:T(8,128)(2,1)S(1)}, u32[]{:S(2)}, u32[]{:S(2)}) collective-permute-start(bf16[512,256]{1,0:T(8,128)(2,1)S(1)} %get-tuple-element.38), channel_id=1, source_target_pairs={{0,32},{1,33},{2,34},{3,35},{4,36},{5,37},{6,38},{7,39},{8,40},{9,... | collective-permute-start | bytes 786440 | tf_op jit(solution)/shard_map/ppermute | solution.py:37
  44.5 5.6 %collective-permute-done.15.arrived_ref = bf16[512,256]{1,0:T(8,128)(2,1)S(1)} collective-permute-done((bf16[512,256]{1,0:T(8,128)(2,1)S(1)}, bf16[512,256]{1,0:T(8,128)(2,1)S(1)}, u32[]{:S(2)}, u32[]{:S(2)}) %collective-permute-start.15) | collective-permute-done | bytes 262176 | tf_op jit(solution)/shard_map/ppermute | solution.py:37
  51.8 2.3 %collective-permute-start.3 = (bf16[2,9,16,256]{3,2,1,0:T(8,128)(2,1)S(1)}, bf16[2,9,16,256]{3,2,1,0:T(8,128)(2,1)S(1)}, u32[]{:S(2)}, u32[]{:S(2)}) collective-permute-start(bf16[2,9,16,256]{3,2,1,0:T(8,128)(2,1)S(1)} %shard_map.122.first_ref), channel_id=1, source_target_pairs={{0,2},{1,3},{2,0},{3,1},{4,6},{5,7},{6,4},{7,5},{8,10},{9,11},{10,... | collective-permute-start | bytes 442376 | tf_op jit(solution)/shard_map/ppermute | solution.py:37
  54.0 5.5 %collective-permute-done.3.second_ref = bf16[2,9,16,256]{3,2,1,0:T(8,128)(2,1)S(1)} collective-permute-done((bf16[2,9,16,256]{3,2,1,0:T(8,128)(2,1)S(1)}, bf16[2,9,16,256]{3,2,1,0:T(8,128)(2,1)S(1)}, u32[]{:S(2)}, u32[]{:S(2)}) %collective-permute-start.3) | collective-permute-done | bytes 147488 | tf_op jit(solution)/shard_map/ppermute | solution.py:37
  59.9 2.1 %collective-permute-start.21 = (bf16[2,2,9,16,256]{4,3,2,1,0:T(8,128)(2,1)S(1)}, bf16[2,2,9,16,256]{4,3,2,1,0:T(8,128)(2,1)S(1)}, u32[]{:S(2)}, u32[]{:S(2)}) collective-permute-start(bf16[2,2,9,16,256]{4,3,2,1,0:T(8,128)(2,1)S(1)} %get-tuple-element.54), channel_id=1, source_target_pairs={{0,4},{1,29},{2,6},{3,31},{4,8},{5,1},{6,10},{7,3},{8,12},{9,5},{1... | collective-permute-start | bytes 884744 | tf_op jit(solution)/shard_map/ppermute | solution.py:37
  62.0 4.6 %collective-permute-start.6 = (bf16[2,9,16,256]{3,2,1,0:T(8,128)(2,1)S(1)}, bf16[2,9,16,256]{3,2,1,0:T(8,128)(2,1)S(1)}, u32[]{:S(2)}, u32[]{:S(2)}) collective-permute-start(bf16[2,9,16,256]{3,2,1,0:T(8,128)(2,1)S(1)} %get-tuple-element.34), channel_id=1, source_target_pairs={{0,8},{1,25},{2,10},{3,27},{4,12},{5,29},{6,14},{7,31},{8,16},{9,1... | collective-permute-start | bytes 442376 | tf_op jit(solution)/shard_map/ppermute | solution.py:37
  68.3 6.2 %collective-permute-done.6.two_ref = bf16[2,9,16,256]{3,2,1,0:T(8,128)(2,1)S(1)} collective-permute-done((bf16[2,9,16,256]{3,2,1,0:T(8,128)(2,1)S(1)}, bf16[2,9,16,256]{3,2,1,0:T(8,128)(2,1)S(1)}, u32[]{:S(2)}, u32[]{:S(2)}) %collective-permute-start.6) | collective-permute-done | bytes 147488 | tf_op jit(solution)/shard_map/ppermute | solution.py:37
  74.5 4.2 %collective-permute-done.22.two_ref = bf16[2,9,16,256]{3,2,1,0:T(8,128)(2,1)S(1)} collective-permute-done((bf16[2,9,16,256]{3,2,1,0:T(8,128)(2,1)S(1)}, bf16[2,9,16,256]{3,2,1,0:T(8,128)(2,1)S(1)}, u32[]{:S(2)}, u32[]{:S(2)}) %collective-permute-start.22) | collective-permute-done | bytes 147488 | tf_op jit(solution)/shard_map/ppermute | solution.py:37
  80.7 5.8 %collective-permute-done.18.two_ref = bf16[2,9,16,256]{3,2,1,0:T(8,128)(2,1)S(1)} collective-permute-done((bf16[2,9,16,256]{3,2,1,0:T(8,128)(2,1)S(1)}, bf16[2,9,16,256]{3,2,1,0:T(8,128)(2,1)S(1)}, u32[]{:S(2)}, u32[]{:S(2)}) %collective-permute-start.18) | collective-permute-done | bytes 147488 | tf_op jit(solution)/shard_map/ppermute | solution.py:37
  87.5 2.4 %collective-permute-start.8 = (bf16[512,256]{1,0:T(8,128)(2,1)S(1)}, bf16[512,256]{1,0:T(8,128)(2,1)S(1)}, u32[]{:S(2)}, u32[]{:S(2)}) collective-permute-start(bf16[512,256]{1,0:T(8,128)(2,1)S(1)} %shard_map.125), channel_id=1, source_target_pairs={{0,32},{1,33},{2,34},{3,35},{4,36},{5,37},{6,38},{7,39},{8,40},{9,... | collective-permute-start | bytes 786440 | tf_op jit(solution)/shard_map/ppermute | solution.py:37
  90.0 2.5 %collective-permute-start.25 = (bf16[2,9,16,256]{3,2,1,0:T(8,128)(2,1)S(1)}, bf16[2,9,16,256]{3,2,1,0:T(8,128)(2,1)S(1)}, u32[]{:S(2)}, u32[]{:S(2)}) collective-permute-start(bf16[2,9,16,256]{3,2,1,0:T(8,128)(2,1)S(1)} %shard_map.141), channel_id=1, source_target_pairs={{0,224},{1,226},{2,225},{3,227},{4,228},{5,230},{6,229},{7,231},{8... | collective-permute-start | bytes 442376 | tf_op jit(solution)/shard_map/ppermute | solution.py:37
  92.5 9.6 %collective-permute-done.25.got_ref = bf16[2,9,16,256]{3,2,1,0:T(8,128)(2,1)S(1)} collective-permute-done((bf16[2,9,16,256]{3,2,1,0:T(8,128)(2,1)S(1)}, bf16[2,9,16,256]{3,2,1,0:T(8,128)(2,1)S(1)}, u32[]{:S(2)}, u32[]{:S(2)}) %collective-permute-start.25) | collective-permute-done | bytes 147488 | tf_op jit(solution)/shard_map/ppermute | solution.py:37
  102.8 1.6 %shard_map.126 = f32[512,256]{1,0:T(8,128)} custom-call(bf16[512,256]{1,0:T(8,128)(2,1)S(1)} %collective-permute-done.8.arrived_ref, f32[512,256]{1,0:T(8,128)S(1)} %bitcast.23, bf16[9,256,256]{2,1,0:T(8,128)(2,1)S(1)} %bitcast.17), custom_call_target="tpu_custom_call" | custom-call | flops 603979776 | bytes 2490368 | tf_op jit(solution)/shard_map/pallas_call | solution.py:88
  104.5 3.7 %collective-permute-start.27 = (bf16[9,8,256]{2,1,0:T(8,128)(2,1)S(1)}, bf16[9,8,256]{2,1,0:T(8,128)(2,1)S(1)}, u32[]{:S(2)}, u32[]{:S(2)}) collective-permute-start(bf16[9,8,256]{2,1,0:T(8,128)(2,1)S(1)} %get-tuple-element.62), channel_id=1, source_target_pairs={{0,16},{1,17},{2,18},{3,19},{4,20},{5,21},{6,22},{7,23},{8,24},{9,... | collective-permute-start | bytes 110600 | tf_op jit(solution)/shard_map/ppermute | solution.py:37
  108.1 1.6 %shard_map.134 = f32[512,256]{1,0:T(8,128)} custom-call(f32[512,256]{1,0:T(8,128)S(1)} %get-tuple-element.43.cot_ref, bf16[576,256]{1,0:T(8,128)(2,1)S(1)} %get-tuple-element.44.dpad_ref, bf16[9,256,256]{2,1,0:T(8,128)(2,1)S(1)} %bitcast.15), custom_call_target="tpu_custom_call" | custom-call | flops 603979776 | bytes 2523136 | tf_op jit(solution)/shard_map/pallas_call | solution.py:88
  109.7 2.7 %collective-permute-done.27 = bf16[9,8,256]{2,1,0:T(8,128)(2,1)S(1)} collective-permute-done((bf16[9,8,256]{2,1,0:T(8,128)(2,1)S(1)}, bf16[9,8,256]{2,1,0:T(8,128)(2,1)S(1)}, u32[]{:S(2)}, u32[]{:S(2)}) %collective-permute-start.27) | collective-permute-done | bytes 36896 | tf_op jit(solution)/shard_map/ppermute | solution.py:37
  (76 shorter events, 18.4 us)
Async XLA Ops:
  1.5 8.2 %collective-permute-start.1 = (bf16[9,8,256]{2,1,0:T(8,128)(2,1)S(1)}, bf16[9,8,256]{2,1,0:T(8,128)(2,1)S(1)}, u32[]{:S(2)}, u32[]{:S(2)}) collective-permute-start(bf16[9,8,256]{2,1,0:T(8,128)(2,1)S(1)} %bitcast.24), channel_id=1, source_target_pairs={{0,16},{1,17},{2,18},{3,19},{4,20},{5,21},{6,22},{7,23},{8,24},{9,... | collective-permute-start | bytes 110600 | tf_op jit(solution)/shard_map/ppermute | solution.py:37
  11.0 7.4 %collective-permute-start.9 = (bf16[2,9,16,256]{3,2,1,0:T(8,128)(2,1)S(1)}, bf16[2,9,16,256]{3,2,1,0:T(8,128)(2,1)S(1)}, u32[]{:S(2)}, u32[]{:S(2)}) collective-permute-start(bf16[2,9,16,256]{3,2,1,0:T(8,128)(2,1)S(1)} %shard_map.122.first_ref), channel_id=1, source_target_pairs={{0,224},{1,227},{2,226},{3,225},{4,228},{5,231},{6,230},{7,229},{8... | collective-permute-start | bytes 442376 | tf_op jit(solution)/shard_map/ppermute | solution.py:37
  19.8 6.8 %collective-permute-start.11 = (bf16[2,2,9,16,256]{4,3,2,1,0:T(8,128)(2,1)S(1)}, bf16[2,2,9,16,256]{4,3,2,1,0:T(8,128)(2,1)S(1)}, u32[]{:S(2)}, u32[]{:S(2)}) collective-permute-start(bf16[2,2,9,16,256]{4,3,2,1,0:T(8,128)(2,1)S(1)} %get-tuple-element.36.chunk_ref), channel_id=1, source_target_pairs={{0,4},{1,29},{2,6},{3,31},{4,8},{5,1},{6,10},{7,3},{8,12},{9,5},{1... | collective-permute-start | bytes 884744 | tf_op jit(solution)/shard_map/ppermute | solution.py:37
  21.6 10.4 %collective-permute-start.13 = (bf16[2,9,16,256]{3,2,1,0:T(8,128)(2,1)S(1)}, bf16[2,9,16,256]{3,2,1,0:T(8,128)(2,1)S(1)}, u32[]{:S(2)}, u32[]{:S(2)}) collective-permute-start(bf16[2,9,16,256]{3,2,1,0:T(8,128)(2,1)S(1)} %get-tuple-element.37), channel_id=1, source_target_pairs={{0,8},{1,25},{2,10},{3,27},{4,12},{5,29},{6,14},{7,31},{8,16},{9,1... | collective-permute-start | bytes 442376 | tf_op jit(solution)/shard_map/ppermute | solution.py:37
  26.6 8.3 %collective-permute-start.12 = (bf16[2,2,9,16,256]{4,3,2,1,0:T(8,128)(2,1)S(1)}, bf16[2,2,9,16,256]{4,3,2,1,0:T(8,128)(2,1)S(1)}, u32[]{:S(2)}, u32[]{:S(2)}) collective-permute-start(bf16[2,2,9,16,256]{4,3,2,1,0:T(8,128)(2,1)S(1)} %collective-permute-done.11.one_ref), channel_id=1, source_target_pairs={{0,1},{1,0},{2,3},{3,2},{4,5},{5,4},{6,7},{7,6},{8,9},{9,8},{10,11... | collective-permute-start | bytes 884744 | tf_op jit(solution)/shard_map/ppermute | solution.py:37
  31.9 3.0 %collective-permute-start.14 = (bf16[2,9,16,256]{3,2,1,0:T(8,128)(2,1)S(1)}, bf16[2,9,16,256]{3,2,1,0:T(8,128)(2,1)S(1)}, u32[]{:S(2)}, u32[]{:S(2)}) collective-permute-start(bf16[2,9,16,256]{3,2,1,0:T(8,128)(2,1)S(1)} %collective-permute-done.13.two_ref), channel_id=1, source_target_pairs={{0,1},{1,0},{2,3},{3,2},{4,5},{5,4},{6,7},{7,6},{8,9},{9,8},{10,11... | collective-permute-start | bytes 442376 | tf_op jit(solution)/shard_map/ppermute | solution.py:37
  38.6 11.5 %collective-permute-start.15 = (bf16[512,256]{1,0:T(8,128)(2,1)S(1)}, bf16[512,256]{1,0:T(8,128)(2,1)S(1)}, u32[]{:S(2)}, u32[]{:S(2)}) collective-permute-start(bf16[512,256]{1,0:T(8,128)(2,1)S(1)} %get-tuple-element.38), channel_id=1, source_target_pairs={{0,32},{1,33},{2,34},{3,35},{4,36},{5,37},{6,38},{7,39},{8,40},{9,... | collective-permute-start | bytes 786440 | tf_op jit(solution)/shard_map/ppermute | solution.py:37
  41.9 17.9 %collective-permute-start.20 = (bf16[8,9,16,256]{3,2,1,0:T(8,128)(2,1)S(1)}, bf16[8,9,16,256]{3,2,1,0:T(8,128)(2,1)S(1)}, u32[]{:S(2)}, u32[]{:S(2)}) collective-permute-start(bf16[8,9,16,256]{3,2,1,0:T(8,128)(2,1)S(1)} %get-tuple-element.53), channel_id=1, source_target_pairs={{0,1},{1,0},{2,3},{3,2},{4,5},{5,4},{6,7},{7,6},{8,9},{9,8},{10,11... | collective-permute-start | bytes 1769480 | tf_op jit(solution)/shard_map/ppermute | solution.py:37
  51.6 15.3 %collective-permute-start.16 = (bf16[8,9,16,256]{3,2,1,0:T(8,128)(2,1)S(1)}, bf16[8,9,16,256]{3,2,1,0:T(8,128)(2,1)S(1)}, u32[]{:S(2)}, u32[]{:S(2)}) collective-permute-start(bf16[8,9,16,256]{3,2,1,0:T(8,128)(2,1)S(1)} %get-tuple-element.46), channel_id=1, source_target_pairs={{0,1},{1,0},{2,3},{3,2},{4,5},{5,4},{6,7},{7,6},{8,9},{9,8},{10,11... | collective-permute-start | bytes 1769480 | tf_op jit(solution)/shard_map/ppermute | solution.py:37
  51.8 7.8 %collective-permute-start.3 = (bf16[2,9,16,256]{3,2,1,0:T(8,128)(2,1)S(1)}, bf16[2,9,16,256]{3,2,1,0:T(8,128)(2,1)S(1)}, u32[]{:S(2)}, u32[]{:S(2)}) collective-permute-start(bf16[2,9,16,256]{3,2,1,0:T(8,128)(2,1)S(1)} %shard_map.122.first_ref), channel_id=1, source_target_pairs={{0,2},{1,3},{2,0},{3,1},{4,6},{5,7},{6,4},{7,5},{8,10},{9,11},{10,... | collective-permute-start | bytes 442376 | tf_op jit(solution)/shard_map/ppermute | solution.py:37
  59.6 7.4 %collective-permute-start.4 = (bf16[2,2,9,16,256]{4,3,2,1,0:T(8,128)(2,1)S(1)}, bf16[2,2,9,16,256]{4,3,2,1,0:T(8,128)(2,1)S(1)}, u32[]{:S(2)}, u32[]{:S(2)}) collective-permute-start(bf16[2,2,9,16,256]{4,3,2,1,0:T(8,128)(2,1)S(1)} %get-tuple-element.33.chunk_ref), channel_id=1, source_target_pairs={{0,4},{1,29},{2,6},{3,31},{4,8},{5,1},{6,10},{7,3},{8,12},{9,5},{1... | collective-permute-start | bytes 884744 | tf_op jit(solution)/shard_map/ppermute | solution.py:37
  59.9 18.8 %collective-permute-start.21 = (bf16[2,2,9,16,256]{4,3,2,1,0:T(8,128)(2,1)S(1)}, bf16[2,2,9,16,256]{4,3,2,1,0:T(8,128)(2,1)S(1)}, u32[]{:S(2)}, u32[]{:S(2)}) collective-permute-start(bf16[2,2,9,16,256]{4,3,2,1,0:T(8,128)(2,1)S(1)} %get-tuple-element.54), channel_id=1, source_target_pairs={{0,4},{1,29},{2,6},{3,31},{4,8},{5,1},{6,10},{7,3},{8,12},{9,5},{1... | collective-permute-start | bytes 884744 | tf_op jit(solution)/shard_map/ppermute | solution.py:37
  62.0 12.5 %collective-permute-start.6 = (bf16[2,9,16,256]{3,2,1,0:T(8,128)(2,1)S(1)}, bf16[2,9,16,256]{3,2,1,0:T(8,128)(2,1)S(1)}, u32[]{:S(2)}, u32[]{:S(2)}) collective-permute-start(bf16[2,9,16,256]{3,2,1,0:T(8,128)(2,1)S(1)} %get-tuple-element.34), channel_id=1, source_target_pairs={{0,8},{1,25},{2,10},{3,27},{4,12},{5,29},{6,14},{7,31},{8,16},{9,1... | collective-permute-start | bytes 442376 | tf_op jit(solution)/shard_map/ppermute | solution.py:37
  66.6 12.1 %collective-permute-start.22 = (bf16[2,9,16,256]{3,2,1,0:T(8,128)(2,1)S(1)}, bf16[2,9,16,256]{3,2,1,0:T(8,128)(2,1)S(1)}, u32[]{:S(2)}, u32[]{:S(2)}) collective-permute-start(bf16[2,9,16,256]{3,2,1,0:T(8,128)(2,1)S(1)} %get-tuple-element.55), channel_id=1, source_target_pairs={{0,8},{1,25},{2,10},{3,27},{4,12},{5,29},{6,14},{7,31},{8,16},{9,1... | collective-permute-start | bytes 442376 | tf_op jit(solution)/shard_map/ppermute | solution.py:37
  67.0 12.1 %collective-permute-start.5 = (bf16[2,2,9,16,256]{4,3,2,1,0:T(8,128)(2,1)S(1)}, bf16[2,2,9,16,256]{4,3,2,1,0:T(8,128)(2,1)S(1)}, u32[]{:S(2)}, u32[]{:S(2)}) collective-permute-start(bf16[2,2,9,16,256]{4,3,2,1,0:T(8,128)(2,1)S(1)} %collective-permute-done.4.one_ref), channel_id=1, source_target_pairs={{0,1},{1,0},{2,3},{3,2},{4,5},{5,4},{6,7},{7,6},{8,9},{9,8},{10,11... | collective-permute-start | bytes 884744 | tf_op jit(solution)/shard_map/ppermute | solution.py:37
  67.1 19.4 %collective-permute-start.17 = (bf16[2,2,9,16,256]{4,3,2,1,0:T(8,128)(2,1)S(1)}, bf16[2,2,9,16,256]{4,3,2,1,0:T(8,128)(2,1)S(1)}, u32[]{:S(2)}, u32[]{:S(2)}) collective-permute-start(bf16[2,2,9,16,256]{4,3,2,1,0:T(8,128)(2,1)S(1)} %get-tuple-element.47), channel_id=1, source_target_pairs={{0,4},{1,29},{2,6},{3,31},{4,8},{5,1},{6,10},{7,3},{8,12},{9,5},{1... | collective-permute-start | bytes 884744 | tf_op jit(solution)/shard_map/ppermute | solution.py:37
  74.5 4.6 %collective-permute-start.7 = (bf16[2,9,16,256]{3,2,1,0:T(8,128)(2,1)S(1)}, bf16[2,9,16,256]{3,2,1,0:T(8,128)(2,1)S(1)}, u32[]{:S(2)}, u32[]{:S(2)}) collective-permute-start(bf16[2,9,16,256]{3,2,1,0:T(8,128)(2,1)S(1)} %collective-permute-done.6.two_ref), channel_id=1, source_target_pairs={{0,1},{1,0},{2,3},{3,2},{4,5},{5,4},{6,7},{7,6},{8,9},{9,8},{10,11... | collective-permute-start | bytes 442376 | tf_op jit(solution)/shard_map/ppermute | solution.py:37
  78.9 7.7 %collective-permute-start.18 = (bf16[2,9,16,256]{3,2,1,0:T(8,128)(2,1)S(1)}, bf16[2,9,16,256]{3,2,1,0:T(8,128)(2,1)S(1)}, u32[]{:S(2)}, u32[]{:S(2)}) collective-permute-start(bf16[2,9,16,256]{3,2,1,0:T(8,128)(2,1)S(1)} %get-tuple-element.48), channel_id=1, source_target_pairs={{0,8},{1,25},{2,10},{3,27},{4,12},{5,29},{6,14},{7,31},{8,16},{9,1... | collective-permute-start | bytes 442376 | tf_op jit(solution)/shard_map/ppermute | solution.py:37
  80.3 9.6 %collective-permute-start.24 = (bf16[2,9,16,256]{3,2,1,0:T(8,128)(2,1)S(1)}, bf16[2,9,16,256]{3,2,1,0:T(8,128)(2,1)S(1)}, u32[]{:S(2)}, u32[]{:S(2)}) collective-permute-start(bf16[2,9,16,256]{3,2,1,0:T(8,128)(2,1)S(1)} %shard_map.140), channel_id=1, source_target_pairs={{0,224},{1,225},{2,226},{3,227},{4,228},{5,229},{6,230},{7,231},{8... | collective-permute-start | bytes 442376 | tf_op jit(solution)/shard_map/ppermute | solution.py:37
  86.6 3.3 %collective-permute-start.19 = (bf16[2,9,16,256]{3,2,1,0:T(8,128)(2,1)S(1)}, bf16[2,9,16,256]{3,2,1,0:T(8,128)(2,1)S(1)}, u32[]{:S(2)}, u32[]{:S(2)}) collective-permute-start(bf16[2,9,16,256]{3,2,1,0:T(8,128)(2,1)S(1)} %get-tuple-element.51), channel_id=1, source_target_pairs={{0,1},{1,0},{2,3},{3,2},{4,5},{5,4},{6,7},{7,6},{8,9},{9,8},{10,11... | collective-permute-start | bytes 442376 | tf_op jit(solution)/shard_map/ppermute | solution.py:37
  87.5 15.3 %collective-permute-start.8 = (bf16[512,256]{1,0:T(8,128)(2,1)S(1)}, bf16[512,256]{1,0:T(8,128)(2,1)S(1)}, u32[]{:S(2)}, u32[]{:S(2)}) collective-permute-start(bf16[512,256]{1,0:T(8,128)(2,1)S(1)} %shard_map.125), channel_id=1, source_target_pairs={{0,32},{1,33},{2,34},{3,35},{4,36},{5,37},{6,38},{7,39},{8,40},{9,... | collective-permute-start | bytes 786440 | tf_op jit(solution)/shard_map/ppermute | solution.py:37
  90.0 12.2 %collective-permute-start.25 = (bf16[2,9,16,256]{3,2,1,0:T(8,128)(2,1)S(1)}, bf16[2,9,16,256]{3,2,1,0:T(8,128)(2,1)S(1)}, u32[]{:S(2)}, u32[]{:S(2)}) collective-permute-start(bf16[2,9,16,256]{3,2,1,0:T(8,128)(2,1)S(1)} %shard_map.141), channel_id=1, source_target_pairs={{0,224},{1,226},{2,225},{3,227},{4,228},{5,230},{6,229},{7,231},{8... | collective-permute-start | bytes 442376 | tf_op jit(solution)/shard_map/ppermute | solution.py:37
  102.2 2.2 %collective-permute-start.26 = (bf16[2,9,8,256]{3,2,1,0:T(8,128)(2,1)S(1)}, bf16[2,9,8,256]{3,2,1,0:T(8,128)(2,1)S(1)}, u32[]{:S(2)}, u32[]{:S(2)}) collective-permute-start(bf16[2,9,8,256]{3,2,1,0:T(8,128)(2,1)S(1)} %get-tuple-element.60), channel_id=1, source_target_pairs={{0,1},{1,0},{2,3},{3,2},{4,5},{5,4},{6,7},{7,6},{8,9},{9,8},{10,11... | collective-permute-start | bytes 221192 | tf_op jit(solution)/shard_map/ppermute | solution.py:37
  104.5 8.0 %collective-permute-start.27 = (bf16[9,8,256]{2,1,0:T(8,128)(2,1)S(1)}, bf16[9,8,256]{2,1,0:T(8,128)(2,1)S(1)}, u32[]{:S(2)}, u32[]{:S(2)}) collective-permute-start(bf16[9,8,256]{2,1,0:T(8,128)(2,1)S(1)} %get-tuple-element.62), channel_id=1, source_target_pairs={{0,16},{1,17},{2,18},{3,19},{4,20},{5,21},{6,22},{7,23},{8,24},{9,... | collective-permute-start | bytes 110600 | tf_op jit(solution)/shard_map/ppermute | solution.py:37
  (13 other events, 59.9 us)
